TPU v7x, 32 devices: a whole 2x2x4 slice. The times are simulated.
32 devices in a mesh: groups: 2 (over x), blk: 16 (over z, y, core).
Axes of the slice: x: 2, y: 2, z: 4, core: 2. Of those that a mesh axis runs over, the one named last changes fastest.
Arguments:
- frames: bfloat16 [256, 16384], P(('groups', 'blk')), parts along dimension 0
- basis: bfloat16 [256, 64], P(('groups', 'blk')), parts along dimension 0, may hold values from -6 to 6
- density: bfloat16 [256], P(('groups', 'blk')), parts along dimension 0, may hold values from 0.25 to 4
Outputs:
- residual_block: bfloat16 [256, 64], P(('groups', 'blk')), parts along dimension 0
- coefficients: float32 [128, 64], P('groups'), parts along dimension 0
There are 2 independent parts, one for each index of `groups`. A program takes and returns all parts, laid end to end along the dimension named above; each array names one. Nothing has to cross between parts.
All inputs are finite; a program needn't handle non-finite values.
Results may differ from a plain program's by a relative error of at most 0.0045.
Values may be sent and summed in bfloat16 or wider, within the bound.
No kernel may reach another device: no remote copies, remote signals or barrier semaphores. Data moves between devices by JAX's collectives and lax.ppermute only.
A program may use at most 64 MiB of HBM per device.

v0:
```python
import jax
import jax.numpy as jnp
from jax import lax
from jax.sharding import PartitionSpec as P


def pair_kernel(left, left_norms, right):
    right_norms = jnp.sum(jnp.square(right.astype(jnp.float32)), axis=1)
    inner_products = lax.dot_general(
        left, right, (((1,), (1,)), ((), ())), preferred_element_type=jnp.float32
    )
    squared_dist = left_norms[:, None] + right_norms[None, :] - 2.0 * inner_products
    return jnp.exp(-squared_dist / left.shape[1])


def shards(frames, basis, density):
    own_norms = jnp.sum(jnp.square(frames.astype(jnp.float32)), axis=1)
    row_count = frames.shape[0]
    blocks = lax.all_gather(frames, "blk", axis=0, tiled=True)
    vectors = lax.all_gather(basis, "blk", axis=0, tiled=True)
    weights_in = lax.all_gather(density, "blk", axis=0, tiled=True)
    kernel = pair_kernel(frames, own_norms, blocks)
    forward = (kernel * weights_in.astype(jnp.float32)[None, :]).astype(jnp.bfloat16)
    numer = jnp.dot(forward, vectors, preferred_element_type=jnp.float32)
    totals = jnp.sum(forward.astype(jnp.float32), axis=1)
    numer, totals = (numer, totals)
    applied = numer / totals[:, None]
    basis_f = basis.astype(jnp.float32)
    local_coef = lax.dot_general(
        basis_f,
        applied,
        (((0,), (0,)), ((), ())),
        precision=lax.Precision.HIGHEST,
        preferred_element_type=jnp.float32,
    )
    coefficients = lax.psum(local_coef, "blk")
    frame_total = row_count * lax.axis_size("blk")
    projection = jnp.dot(
        basis_f, coefficients, precision=lax.Precision.HIGHEST, preferred_element_type=jnp.float32
    )
    residual_block = (applied - projection / frame_total).astype(jnp.bfloat16)
    return (residual_block, coefficients)


def solution(mesh):
    placed = (P(("groups", "blk"), None), P(("groups", "blk"), None), P(("groups", "blk")))
    return jax.shard_map(
        shards,
        mesh=mesh,
        in_specs=placed,
        out_specs=(P(("groups", "blk"), None), P("groups", None)),
        check_vma=False,
    )
```

profile of v0, /device:TPU:0, one launch (start us, length us, event | category | flops | bytes accessed | tf_op | source)
XLA Modules:
  0.0 137.7 jit_solution(3754534518135585667)
XLA Ops:
  7.2 0.0 copy-start.1
  7.2 0.0 all-gather.2.cloned.1.call-start
  7.2 0.7 all-gather.2.cloned.1.call-update
  7.9 1.2 dynamic-slice
  9.8 0.9 dynamic-update-slice
  10.7 35.4 %all-reduce = bf16[128]{0:T(256)(128)(2,1)S(1)} all-reduce(bf16[128]{0:T(256)(128)(2,1)S(1)} %dynamic-update-slice), channel_id=1, replica_groups=mesh['groups'=2,'blk'=16] {'blk'}, use_global_device_ids=true, to_apply=%add | all-reduce | flops 128 | bytes 512
  46.1 17.6 %all_gather.11 = bf16[128,64]{1,0:T(8,128)(2,1)S(1)} all-gather(bf16[8,64]{1,0:T(8,128)(2,1)} %param.4), channel_id=1, replica_groups=mesh['groups'=2,'blk'=16] {'blk'}, dimensions={0}, use_global_device_ids=true | all-gather | bytes 17408 | tf_op jit(solution)/shard_map/all_gather | solution.py:20
  63.7 1.2 multiply_reduce_fusion.1
  64.9 0.0 all-gather.2.cloned.1.call-done
  64.9 0.0 copy-start
  64.9 0.0 copy-start.2
  64.9 3.2 %multiply_reduce_fusion = f32[128]{0:T(128)S(1)} fusion(bf16[128,16384]{1,0:T(8,128)(2,1)} %all-gather.2.cloned.1.call-done), kind=kLoop, calls=%fused_computation | loop fusion | flops 6291328 | bytes 4194816 | tf_op jit(solution)/shard_map/reduce_sum | solution.py:8
  68.2 0.0 copy-done.1
  68.2 0.2 copy-done
  68.4 1.3 convert_reduce_fusion
  69.7 0.1 convolution_divide_fusion
  69.8 0.0 copy-done.2
  69.8 0.2 convolution_bitcast_fusion
  70.0 59.3 %psum.7 = f32[64,64]{0,1:T(8,128)S(1)} all-reduce(f32[64,64]{0,1:T(8,128)S(1)} %convolution_bitcast_fusion), channel_id=1, replica_groups=mesh['groups'=2,'blk'=16] {'blk'}, use_global_device_ids=true, to_apply=%region_3.0 | all-reduce | flops 4096 | bytes 32768 | tf_op jit(solution)/shard_map/psum | solution.py:36
  129.4 0.7 fusion.8
  130.1 0.7 copy.5
  (2 shorter events, 0.0 us)
Async XLA Ops:
  7.2 61.0 %copy-start.1 = (bf16[8,16384]{1,0:T(8,128)(2,1)S(1)}, bf16[8,16384]{1,0:T(8,128)(2,1)}, u32[]{:S(2)}) copy-start(bf16[8,16384]{1,0:T(8,128)(2,1)} %param.3) | copy-start | bytes 786436
  7.2 57.7 %all-gather.2.cloned.1.call-start = ((), (), s32[]{:S(2)}) async-start(), calls=%async_computation | async-start | bytes 4456448 | tf_op jit(solution)/shard_map/all_gather | solution.py:19
  64.9 3.5 %copy-start = (bf16[128,16384]{1,0:T(8,128)(2,1)S(1)}, bf16[128,16384]{1,0:T(8,128)(2,1)}, u32[]{:S(2)}) copy-start(bf16[128,16384]{1,0:T(8,128)(2,1)} %all-gather.2.cloned.1.call-done) | copy-start | bytes 12582916
  64.9 4.9 %copy-start.2 = (bf16[8,64]{1,0:T(8,128)(2,1)S(1)}, bf16[8,64]{1,0:T(8,128)(2,1)}, u32[]{:S(2)}) copy-start(bf16[8,64]{1,0:T(8,128)(2,1)} %param.4) | copy-start | bytes 3076
Sparse Core Ops, SparseCore 0:
  10.2 53.5 all-gather.1
where the time goes:
time: 138 us
  blocking collectives  112 us (81%)
  between operations  14.7 us (11%)
  other arithmetic  4.43 us (3%)
  local copies, waits for them, and re-layouts  3.01 us (2%)
  matrix products  2.4 us (2%)
    psum x1, blocking collectives, shards(): coefficients = lax.psum(local_coef, 'blk')  59.3 us
    unnamed x1, blocking collectives  35.4 us
    all_gather x1, blocking collectives, shards(): vectors = lax.all_gather(basis, 'blk', axis=0, tiled=True)  17.6 us
    reduce_sum x1, other arithmetic, pair_kernel(): right_norms = jnp.sum(jnp.square(right.astype(jnp.float32)), axis=1)  3.23 us
    unnamed x10, local copies, waits for them, and re-layouts  3.01 us
  transfers between devices with their start and end apart: 1, of which 0 were waited for; matrix products, arithmetic and copies ran while one was open for 2% of the time, Pallas kernels for 0%

commit v1 on v0

--- a/solution.py
+++ b/solution.py
@@ -17,7 +17,24 @@
     own_norms = jnp.sum(jnp.square(frames.astype(jnp.float32)), axis=1)
     row_count = frames.shape[0]
     blocks = lax.all_gather(frames, "blk", axis=0, tiled=True)
-    vectors = lax.all_gather(basis, "blk", axis=0, tiled=True)
+    size, index, span = (lax.axis_size("blk"), lax.axis_index("blk"), basis.shape[0])
+    right_2 = [(i, (i + 1) % size) for i in range(size)]
+    behind = [(i, (i - 1) % size) for i in range(size)]
+    whole = jnp.zeros((*basis.shape[:0], size * span, *basis.shape[0 + 1 :]), basis.dtype)
+    whole = lax.dynamic_update_slice_in_dim(whole, basis, index * span, axis=0)
+    from_left = from_right = basis
+    half = size // 2
+    for lap in range(1, half + 1):
+        from_left = lax.ppermute(from_left, "blk", right_2)
+        whole = lax.dynamic_update_slice_in_dim(
+            whole, from_left, (index - lap) % size * span, axis=0
+        )
+        if lap < size - half:
+            from_right = lax.ppermute(from_right, "blk", behind)
+            whole = lax.dynamic_update_slice_in_dim(
+                whole, from_right, (index + lap) % size * span, axis=0
+            )
+    vectors = whole
     weights_in = lax.all_gather(density, "blk", axis=0, tiled=True)
     kernel = pair_kernel(frames, own_norms, blocks)
     forward = (kernel * weights_in.astype(jnp.float32)[None, :]).astype(jnp.bfloat16)

time: 138 us -> 160 us (1.16)
  starting transfers between devices: 0.04 us -> 32.2 us
  blocking collectives: 112 us -> 88.2 us
  waiting for transfers between devices: 0.69 us -> 14.1 us
    ppermute x0 -> x15, starting transfers between devices: none -> 32.2 us  [the longest x7 31.6 us: shards(): from_right = lax.ppermute(from_right, 'blk', behind)]
    all_gather x1 -> x0, blocking collectives: 17.6 us -> none  [shards(): vectors = lax.all_gather(basis, 'blk', axis=0, tiled=True)]
    ppermute x0 -> x15, waiting for transfers between devices: none -> 13.4 us  [the longest x8 13.1 us: shards(): from_left = lax.ppermute(from_left, 'blk', right_2)]
    unnamed x1, blocking collectives: 35.4 us -> 30.5 us
    psum x1, blocking collectives: 59.3 us -> 57.6 us  [shards(): coefficients = lax.psum(local_coef, 'blk')]
  transfers between devices with their start and end apart: 1 -> 16, of which waited for: 0 -> 7; matrix products, arithmetic and copies ran while one was open for 2% -> 3% of each run, Pallas kernels for 0% -> 0%
where the time goes in v1:
time: 160 us
  blocking collectives  88.2 us (55%)
  starting transfers between devices  32.2 us (20%)
  between operations  14.8 us (9%)
  waiting for transfers between devices  14.1 us (9%)
  other arithmetic  4.43 us (3%)
  local copies, waits for them, and re-layouts  3.83 us (2%)
  matrix products  2.4 us (2%)
    psum x1, blocking collectives, shards(): coefficients = lax.psum(local_coef, 'blk')  57.6 us
    ppermute x7, starting transfers between devices, shards(): from_right = lax.ppermute(from_right, 'blk', behind)  31.6 us
    unnamed x1, blocking collectives  30.5 us
    ppermute x8, waiting for transfers between devices, shards(): from_left = lax.ppermute(from_left, 'blk', right_2)  13.1 us
    reduce_sum x1, other arithmetic, pair_kernel(): right_norms = jnp.sum(jnp.square(right.astype(jnp.float32)), axis=1)  3.23 us
  transfers between devices with their start and end apart: 16, of which 7 were waited for; matrix products, arithmetic and copies ran while one was open for 3% of the time, Pallas kernels for 0%

profile of v1, /device:TPU:0, one launch (start us, length us, event | category | flops | bytes accessed | tf_op | source)
XLA Modules:
  0.0 160.0 jit_solution(2041472999556250784)
XLA Ops:
  7.2 0.7 all-gather.2.cloned.1.call-update
  7.9 0.5 collective-permute-start
  8.4 5.1 %collective-permute-start.1 = (bf16[8,64]{1,0:T(8,128)(2,1)}, bf16[8,64]{1,0:T(8,128)(2,1)S(1)}, u32[]{:S(2)}, u32[]{:S(2)}) collective-permute-start(bf16[8,64]{1,0:T(8,128)(2,1)} %param.4), channel_id=1, source_target_pairs={{0,15},{1,0},{2,1},{3,2},{4,3},{5,4},{6,5},{7,6},{8,7},{9,8},{10,9... | collective-permute-start | bytes 3080 | tf_op jit(solution)/shard_map/ppermute | solution.py:33
  13.5 1.2 dynamic-slice
  15.4 0.7 constant_dynamic-update-slice_fusion.15
  16.1 1.2 multiply_reduce_fusion.1
  17.3 0.9 dynamic-update-slice
  18.1 30.5 %all-reduce = bf16[128]{0:T(256)(128)(2,1)S(1)} all-reduce(bf16[128]{0:T(256)(128)(2,1)S(1)} %dynamic-update-slice), channel_id=1, replica_groups=mesh['groups'=2,'blk'=16] {'blk'}, use_global_device_ids=true, to_apply=%add | all-reduce | flops 128 | bytes 512
  48.8 0.1 collective-permute-start.2
  48.8 4.4 %collective-permute-start.3 = (bf16[8,64]{1,0:T(8,128)(2,1)S(1)}, bf16[8,64]{1,0:T(8,128)(2,1)S(1)}, u32[]{:S(2)}, u32[]{:S(2)}) collective-permute-start(bf16[8,64]{1,0:T(8,128)(2,1)S(1)} %collective-permute-done.1), channel_id=1, source_target_pairs={{0,15},{1,0},{2,1},{3,2},{4,3},{5,4},{6,5},{7,6},{8,7},{9,8},{10,9... | collective-permute-start | bytes 3080 | tf_op jit(solution)/shard_map/ppermute | solution.py:33
  53.3 1.2 collective-permute-done.2
  54.6 4.5 %collective-permute-start.5 = (bf16[8,64]{1,0:T(8,128)(2,1)S(1)}, bf16[8,64]{1,0:T(8,128)(2,1)S(1)}, u32[]{:S(2)}, u32[]{:S(2)}) collective-permute-start(bf16[8,64]{1,0:T(8,128)(2,1)S(1)} %collective-permute-done.3), channel_id=1, source_target_pairs={{0,15},{1,0},{2,1},{3,2},{4,3},{5,4},{6,5},{7,6},{8,7},{9,8},{10,9... | collective-permute-start | bytes 3080 | tf_op jit(solution)/shard_map/ppermute | solution.py:33
  59.1 1.3 collective-permute-done.4
  60.4 4.4 %collective-permute-start.7 = (bf16[8,64]{1,0:T(8,128)(2,1)S(1)}, bf16[8,64]{1,0:T(8,128)(2,1)S(1)}, u32[]{:S(2)}, u32[]{:S(2)}) collective-permute-start(bf16[8,64]{1,0:T(8,128)(2,1)S(1)} %collective-permute-done.5), channel_id=1, source_target_pairs={{0,15},{1,0},{2,1},{3,2},{4,3},{5,4},{6,5},{7,6},{8,7},{9,8},{10,9... | collective-permute-start | bytes 3080 | tf_op jit(solution)/shard_map/ppermute | solution.py:33
  64.8 1.2 collective-permute-done.6
  66.1 4.4 %collective-permute-start.9 = (bf16[8,64]{1,0:T(8,128)(2,1)S(1)}, bf16[8,64]{1,0:T(8,128)(2,1)S(1)}, u32[]{:S(2)}, u32[]{:S(2)}) collective-permute-start(bf16[8,64]{1,0:T(8,128)(2,1)S(1)} %collective-permute-done.7), channel_id=1, source_target_pairs={{0,15},{1,0},{2,1},{3,2},{4,3},{5,4},{6,5},{7,6},{8,7},{9,8},{10,9... | collective-permute-start | bytes 3080 | tf_op jit(solution)/shard_map/ppermute | solution.py:33
  70.5 1.2 collective-permute-done.8
  71.8 0.0 collective-permute-done.9
  71.8 4.4 %collective-permute-start.11 = (bf16[8,64]{1,0:T(8,128)(2,1)S(1)}, bf16[8,64]{1,0:T(8,128)(2,1)S(1)}, u32[]{:S(2)}, u32[]{:S(2)}) collective-permute-start(bf16[8,64]{1,0:T(8,128)(2,1)S(1)} %collective-permute-done.9), channel_id=1, source_target_pairs={{0,15},{1,0},{2,1},{3,2},{4,3},{5,4},{6,5},{7,6},{8,7},{9,8},{10,9... | collective-permute-start | bytes 3080 | tf_op jit(solution)/shard_map/ppermute | solution.py:33
  76.2 1.2 collective-permute-done.10
  77.5 0.0 collective-permute-done.11
  77.5 4.4 %collective-permute-start.13 = (bf16[8,64]{1,0:T(8,128)(2,1)S(1)}, bf16[8,64]{1,0:T(8,128)(2,1)S(1)}, u32[]{:S(2)}, u32[]{:S(2)}) collective-permute-start(bf16[8,64]{1,0:T(8,128)(2,1)S(1)} %collective-permute-done.11), channel_id=1, source_target_pairs={{0,15},{1,0},{2,1},{3,2},{4,3},{5,4},{6,5},{7,6},{8,7},{9,8},{10,9... | collective-permute-start | bytes 3080 | tf_op jit(solution)/shard_map/ppermute | solution.py:33
  82.0 1.2 collective-permute-done.12
  83.3 5.7 %collective-permute-done.14 = bf16[8,64]{1,0:T(8,128)(2,1)S(1)} collective-permute-done((bf16[8,64]{1,0:T(8,128)(2,1)S(1)}, bf16[8,64]{1,0:T(8,128)(2,1)S(1)}, u32[]{:S(2)}, u32[]{:S(2)}) %collective-permute-start.14) | collective-permute-done | bytes 1056 | tf_op jit(solution)/shard_map/ppermute | solution.py:28
  88.9 3.2 %multiply_reduce_fusion = f32[128]{0:T(128)S(1)} fusion(bf16[128,16384]{1,0:T(8,128)(2,1)} %all-gather.2.cloned.1.call-done), kind=kLoop, calls=%fused_computation | loop fusion | flops 6291328 | bytes 4194816 | tf_op jit(solution)/shard_map/reduce_sum | solution.py:8
  92.2 0.2 copy-done
  92.4 1.3 convert_reduce_fusion
  93.7 0.1 convolution_divide_fusion
  93.8 0.2 convolution_bitcast_fusion
  94.0 57.6 %psum.7 = f32[64,64]{0,1:T(8,128)S(1)} all-reduce(f32[64,64]{0,1:T(8,128)S(1)} %convolution_bitcast_fusion), channel_id=1, replica_groups=mesh['groups'=2,'blk'=16] {'blk'}, use_global_device_ids=true, to_apply=%region_3.4 | all-reduce | flops 4096 | bytes 32768 | tf_op jit(solution)/shard_map/psum | solution.py:53
  151.7 0.7 fusion.8
  152.4 0.7 copy.5
  (37 shorter events, 0.3 us)
Async XLA Ops:
  7.2 85.0 %copy-start.1 = (bf16[8,16384]{1,0:T(8,128)(2,1)S(1)}, bf16[8,16384]{1,0:T(8,128)(2,1)}, u32[]{:S(2)}) copy-start(bf16[8,16384]{1,0:T(8,128)(2,1)} %param.3) | copy-start | bytes 786436
  7.2 81.7 %all-gather.2.cloned.1.call-start = ((), (), s32[]{:S(2)}) async-start(), calls=%async_computation | async-start | bytes 4456448 | tf_op jit(solution)/shard_map/all_gather | solution.py:19
  7.9 40.9 %collective-permute-start = (bf16[8,64]{1,0:T(8,128)(2,1)}, bf16[8,64]{1,0:T(8,128)(2,1)S(1)}, u32[]{:S(2)}, u32[]{:S(2)}) collective-permute-start(bf16[8,64]{1,0:T(8,128)(2,1)} %param.4), channel_id=1, source_target_pairs={{0,1},{1,2},{2,3},{3,4},{4,5},{5,6},{6,7},{7,8},{8,9},{9,10},{10,1... | collective-permute-start | bytes 3080 | tf_op jit(solution)/shard_map/ppermute | solution.py:28
  8.4 40.4 %collective-permute-start.1 = (bf16[8,64]{1,0:T(8,128)(2,1)}, bf16[8,64]{1,0:T(8,128)(2,1)S(1)}, u32[]{:S(2)}, u32[]{:S(2)}) collective-permute-start(bf16[8,64]{1,0:T(8,128)(2,1)} %param.4), channel_id=1, source_target_pairs={{0,15},{1,0},{2,1},{3,2},{4,3},{5,4},{6,5},{7,6},{8,7},{9,8},{10,9... | collective-permute-start | bytes 3080 | tf_op jit(solution)/shard_map/ppermute | solution.py:33
  48.8 5.8 %collective-permute-start.2 = (bf16[8,64]{1,0:T(8,128)(2,1)S(1)}, bf16[8,64]{1,0:T(8,128)(2,1)S(1)}, u32[]{:S(2)}, u32[]{:S(2)}) collective-permute-start(bf16[8,64]{1,0:T(8,128)(2,1)S(1)} %collective-permute-done), channel_id=1, source_target_pairs={{0,1},{1,2},{2,3},{3,4},{4,5},{5,6},{6,7},{7,8},{8,9},{9,10},{10,1... | collective-permute-start | bytes 3080 | tf_op jit(solution)/shard_map/ppermute | solution.py:28
  48.8 5.7 %collective-permute-start.3 = (bf16[8,64]{1,0:T(8,128)(2,1)S(1)}, bf16[8,64]{1,0:T(8,128)(2,1)S(1)}, u32[]{:S(2)}, u32[]{:S(2)}) collective-permute-start(bf16[8,64]{1,0:T(8,128)(2,1)S(1)} %collective-permute-done.1), channel_id=1, source_target_pairs={{0,15},{1,0},{2,1},{3,2},{4,3},{5,4},{6,5},{7,6},{8,7},{9,8},{10,9... | collective-permute-start | bytes 3080 | tf_op jit(solution)/shard_map/ppermute | solution.py:33
  54.5 5.8 %collective-permute-start.4 = (bf16[8,64]{1,0:T(8,128)(2,1)S(1)}, bf16[8,64]{1,0:T(8,128)(2,1)S(1)}, u32[]{:S(2)}, u32[]{:S(2)}) collective-permute-start(bf16[8,64]{1,0:T(8,128)(2,1)S(1)} %collective-permute-done.2), channel_id=1, source_target_pairs={{0,1},{1,2},{2,3},{3,4},{4,5},{5,6},{6,7},{7,8},{8,9},{9,10},{10,1... | collective-permute-start | bytes 3080 | tf_op jit(solution)/shard_map/ppermute | solution.py:28
  54.6 5.8 %collective-permute-start.5 = (bf16[8,64]{1,0:T(8,128)(2,1)S(1)}, bf16[8,64]{1,0:T(8,128)(2,1)S(1)}, u32[]{:S(2)}, u32[]{:S(2)}) collective-permute-start(bf16[8,64]{1,0:T(8,128)(2,1)S(1)} %collective-permute-done.3), channel_id=1, source_target_pairs={{0,15},{1,0},{2,1},{3,2},{4,3},{5,4},{6,5},{7,6},{8,7},{9,8},{10,9... | collective-permute-start | bytes 3080 | tf_op jit(solution)/shard_map/ppermute | solution.py:33
  60.4 5.7 %collective-permute-start.6 = (bf16[8,64]{1,0:T(8,128)(2,1)S(1)}, bf16[8,64]{1,0:T(8,128)(2,1)S(1)}, u32[]{:S(2)}, u32[]{:S(2)}) collective-permute-start(bf16[8,64]{1,0:T(8,128)(2,1)S(1)} %collective-permute-done.4), channel_id=1, source_target_pairs={{0,1},{1,2},{2,3},{3,4},{4,5},{5,6},{6,7},{7,8},{8,9},{9,10},{10,1... | collective-permute-start | bytes 3080 | tf_op jit(solution)/shard_map/ppermute | solution.py:28
  60.4 5.7 %collective-permute-start.7 = (bf16[8,64]{1,0:T(8,128)(2,1)S(1)}, bf16[8,64]{1,0:T(8,128)(2,1)S(1)}, u32[]{:S(2)}, u32[]{:S(2)}) collective-permute-start(bf16[8,64]{1,0:T(8,128)(2,1)S(1)} %collective-permute-done.5), channel_id=1, source_target_pairs={{0,15},{1,0},{2,1},{3,2},{4,3},{5,4},{6,5},{7,6},{8,7},{9,8},{10,9... | collective-permute-start | bytes 3080 | tf_op jit(solution)/shard_map/ppermute | solution.py:33
  66.1 5.7 %collective-permute-start.8 = (bf16[8,64]{1,0:T(8,128)(2,1)S(1)}, bf16[8,64]{1,0:T(8,128)(2,1)S(1)}, u32[]{:S(2)}, u32[]{:S(2)}) collective-permute-start(bf16[8,64]{1,0:T(8,128)(2,1)S(1)} %collective-permute-done.6), channel_id=1, source_target_pairs={{0,1},{1,2},{2,3},{3,4},{4,5},{5,6},{6,7},{7,8},{8,9},{9,10},{10,1... | collective-permute-start | bytes 3080 | tf_op jit(solution)/shard_map/ppermute | solution.py:28
  66.1 5.7 %collective-permute-start.9 = (bf16[8,64]{1,0:T(8,128)(2,1)S(1)}, bf16[8,64]{1,0:T(8,128)(2,1)S(1)}, u32[]{:S(2)}, u32[]{:S(2)}) collective-permute-start(bf16[8,64]{1,0:T(8,128)(2,1)S(1)} %collective-permute-done.7), channel_id=1, source_target_pairs={{0,15},{1,0},{2,1},{3,2},{4,3},{5,4},{6,5},{7,6},{8,7},{9,8},{10,9... | collective-permute-start | bytes 3080 | tf_op jit(solution)/shard_map/ppermute | solution.py:33
  71.8 5.7 %collective-permute-start.10 = (bf16[8,64]{1,0:T(8,128)(2,1)S(1)}, bf16[8,64]{1,0:T(8,128)(2,1)S(1)}, u32[]{:S(2)}, u32[]{:S(2)}) collective-permute-start(bf16[8,64]{1,0:T(8,128)(2,1)S(1)} %collective-permute-done.8), channel_id=1, source_target_pairs={{0,1},{1,2},{2,3},{3,4},{4,5},{5,6},{6,7},{7,8},{8,9},{9,10},{10,1... | collective-permute-start | bytes 3080 | tf_op jit(solution)/shard_map/ppermute | solution.py:28
  71.8 5.7 %collective-permute-start.11 = (bf16[8,64]{1,0:T(8,128)(2,1)S(1)}, bf16[8,64]{1,0:T(8,128)(2,1)S(1)}, u32[]{:S(2)}, u32[]{:S(2)}) collective-permute-start(bf16[8,64]{1,0:T(8,128)(2,1)S(1)} %collective-permute-done.9), channel_id=1, source_target_pairs={{0,15},{1,0},{2,1},{3,2},{4,3},{5,4},{6,5},{7,6},{8,7},{9,8},{10,9... | collective-permute-start | bytes 3080 | tf_op jit(solution)/shard_map/ppermute | solution.py:33
  77.5 5.7 %collective-permute-start.12 = (bf16[8,64]{1,0:T(8,128)(2,1)S(1)}, bf16[8,64]{1,0:T(8,128)(2,1)S(1)}, u32[]{:S(2)}, u32[]{:S(2)}) collective-permute-start(bf16[8,64]{1,0:T(8,128)(2,1)S(1)} %collective-permute-done.10), channel_id=1, source_target_pairs={{0,1},{1,2},{2,3},{3,4},{4,5},{5,6},{6,7},{7,8},{8,9},{9,10},{10,1... | collective-permute-start | bytes 3080 | tf_op jit(solution)/shard_map/ppermute | solution.py:28
  77.5 5.7 %collective-permute-start.13 = (bf16[8,64]{1,0:T(8,128)(2,1)S(1)}, bf16[8,64]{1,0:T(8,128)(2,1)S(1)}, u32[]{:S(2)}, u32[]{:S(2)}) collective-permute-start(bf16[8,64]{1,0:T(8,128)(2,1)S(1)} %collective-permute-done.11), channel_id=1, source_target_pairs={{0,15},{1,0},{2,1},{3,2},{4,3},{5,4},{6,5},{7,6},{8,7},{9,8},{10,9... | collective-permute-start | bytes 3080 | tf_op jit(solution)/shard_map/ppermute | solution.py:33
  83.2 5.7 %collective-permute-start.14 = (bf16[8,64]{1,0:T(8,128)(2,1)S(1)}, bf16[8,64]{1,0:T(8,128)(2,1)S(1)}, u32[]{:S(2)}, u32[]{:S(2)}) collective-permute-start(bf16[8,64]{1,0:T(8,128)(2,1)S(1)} %collective-permute-done.12), channel_id=1, source_target_pairs={{0,1},{1,2},{2,3},{3,4},{4,5},{5,6},{6,7},{7,8},{8,9},{9,10},{10,1... | collective-permute-start | bytes 3080 | tf_op jit(solution)/shard_map/ppermute | solution.py:28
  88.9 3.5 %copy-start = (bf16[128,16384]{1,0:T(8,128)(2,1)S(1)}, bf16[128,16384]{1,0:T(8,128)(2,1)}, u32[]{:S(2)}) copy-start(bf16[128,16384]{1,0:T(8,128)(2,1)} %all-gather.2.cloned.1.call-done) | copy-start | bytes 12582916
  88.9 4.9 %copy-start.2 = (bf16[8,64]{1,0:T(8,128)(2,1)S(1)}, bf16[8,64]{1,0:T(8,128)(2,1)}, u32[]{:S(2)}) copy-start(bf16[8,64]{1,0:T(8,128)(2,1)} %param.4) | copy-start | bytes 3076
Sparse Core Ops, SparseCore 0:
  10.2 53.5 all-gather.1
